TPU v7x, 512 devices: a whole 4x8x8 slice. The times are simulated.
512 devices in a mesh: ket: 128 (over z, y, core), blk: 4 (over x).
Axes of the slice: x: 4, y: 8, z: 8, core: 2. Of those that a mesh axis runs over, the one named last changes fastest.
Arguments:
- density: float32 [8192, 64, 128], P('ket', 'blk'), may hold values from -24 to 24
- decay_matrix: float32 [128, 128], replicated, may hold values from -0.25 to 2, as said below
- atom_order: int32 [128], replicated, may hold values from 0 to 127, each once
Outputs:
- next_vector: float32 [8192, 64, 128], P('ket', 'blk')
- krylov_coeffs: float32 [5], replicated
- jump_flux: float32 [8192], P(('ket', 'blk'))
Inputs may be any that keep to these rules, and one draw needn't show every extreme that they name: `decay_matrix`: symmetric; diagonal entries from 0.5 to 2, off-diagonal entries at most 0.25 in magnitude. `atom_order`: each atom once.
All inputs are finite; a program needn't handle non-finite values.
Results may differ from a plain program's by a relative error of at most 0.0003.
Values sent between devices are 32-bit elements; how exact they have to be, the bound alone decides.
No kernel may reach another device: no remote copies, remote signals or barrier semaphores. Data moves between devices by JAX's collectives and lax.ppermute only.
A program may use at most 64 MiB of HBM per device.

v0:
```python
import jax
import jax.numpy as jnp
from jax import lax
from jax.sharding import PartitionSpec as P

highest = lax.Precision.HIGHEST


def shards(density, decay_matrix, atom_order):
    pair_rows, bra_local, atom_count = density.shape
    block_shape = density.shape
    half = bra_local * lax.axis_size("blk")
    entries = float(atom_count) * float(half) * float(half) * float(atom_count)
    onehot = (atom_order[:, None] == jnp.arange(atom_count)[None, :]).astype(jnp.float32)
    coupling = jnp.dot(
        jnp.dot(onehot, decay_matrix, precision=highest), onehot.T, precision=highest
    )
    window = coupling[:half, :half]

    def ket_part(turned):
        ket_cube = turned.reshape(atom_count, half, -1)
        summed = jnp.einsum("ia,ajc->ijc", coupling, ket_cube, precision=highest) + jnp.einsum(
            "jb,ibc->ijc", window, ket_cube, precision=highest
        )
        return summed.reshape(turned.shape)

    def bra_part(tensor):
        turned = lax.all_to_all(tensor, "blk", split_axis=2, concat_axis=1, tiled=True)
        mixed_rows = jnp.einsum("kb,pbc->pkc", window, turned, precision=highest)
        returned = lax.all_to_all(mixed_rows, "blk", split_axis=1, concat_axis=2, tiled=True)
        return returned + jnp.einsum("ld,pkd->pkl", coupling, tensor, precision=highest)

    def krylov_step(vectors, image_vec):
        local_dots = jnp.stack([jnp.sum(vector * image_vec) for vector in vectors])
        correlation = lax.psum(local_dots, ("ket", "blk")) / entries
        residual = image_vec
        for position in range(len(vectors)):
            residual = residual - correlation[position] * vectors[position]
        length_value = jnp.sqrt(lax.psum(jnp.sum(residual * residual), ("ket", "blk")) / entries)
        return (correlation, length_value, residual / length_value)

    norm_start = lax.psum(jnp.sum(density * density), ("ket", "blk"))
    vector_one = density / jnp.sqrt(norm_start / entries)

    def liouvillian(tensor):
        turned = lax.all_to_all(
            tensor.reshape(pair_rows, -1), "ket", split_axis=1, concat_axis=0, tiled=True
        )
        returned = lax.all_to_all(
            ket_part(turned), "ket", split_axis=0, concat_axis=1, tiled=True
        ).reshape(block_shape)
        return -0.5 * (returned + bra_part(tensor))

    coeff_one, length_one, vector_two = krylov_step([vector_one], liouvillian(vector_one))
    coeff_two, length_two, next_vector = krylov_step(
        [vector_one, vector_two], liouvillian(vector_two)
    )
    krylov_coeffs = jnp.concatenate([coeff_one, length_one[None], coeff_two, length_two[None]])
    pair_start = lax.axis_index("ket") * pair_rows
    pair_ids = pair_start + jnp.arange(pair_rows, dtype=jnp.int32)
    row_atoms = pair_ids // half
    picker = (row_atoms[:, None] == jnp.arange(atom_count)[None, :]).astype(jnp.float32)
    rows_full = jnp.dot(picker, coupling[:, :half], precision=highest)
    weights = lax.dynamic_slice_in_dim(rows_full, lax.axis_index("blk") * bra_local, bra_local, 1)
    summed_rows = jnp.einsum("pb,pbl->pl", weights, density, precision=highest)
    partial_value = summed_rows.reshape(pair_rows // half, half, atom_count).sum(0)
    jump_flux = lax.psum_scatter(
        partial_value.reshape(-1) / atom_count, ("ket", "blk"), scatter_dimension=0, tiled=True
    )
    return (next_vector, krylov_coeffs, jump_flux)


def solution(mesh):
    return jax.shard_map(
        shards,
        mesh=mesh,
        in_specs=(P("ket", "blk", None), P(), P()),
        out_specs=(P("ket", "blk", None), P(), P(("ket", "blk"))),
        check_vma=False,
    )
```

profile of v0, /device:TPU:1, one launch (start us, length us, event | category | flops | bytes accessed | tf_op | source)
XLA Modules:
  0.0 683.4 jit_solution(7631907614733165362)
XLA Ops:
  2.5 106.0 %psum.35 = f32[]{:T(128)} all-reduce(f32[]{:T(128)} %multiply_reduce_fusion.5), channel_id=1, replica_groups=mesh['ket'=128,'blk'=4] {'ket','blk'}, use_global_device_ids=true, to_apply=%region_1.0 | all-reduce | flops 1 | bytes 8 | tf_op jit(solution)/shard_map/psum | solution.py:42
  111.3 3.5 all-to-all-start.2
  116.6 7.1 %all-to-all-done.2 = f32[4,1,32768]{2,1,0:T(1,128)S(1)} async-done(((f32[4,1,32768]{2,1,0:T(1,128)}), f32[4,1,32768]{2,1,0:T(1,128)S(1)}, u32[]{:S(2)}, u32[]{:S(2)}) %all-to-all-start.2) | async-done | bytes 524320 | tf_op jit(solution)/shard_map/all_to_all | solution.py:28
  123.7 10.5 %all-to-all-start = ((f32[128,1,1024]{2,1,0:T(1,128)}), f32[128,1,1024]{2,1,0:T(1,128)}, u32[]{:S(2)}, u32[]{:S(2)}) async-start(f32[128,1,1024]{2,1,0:T(1,128)} %reshape.77), calls=%async_computation | async-start | bytes 1048576 | tf_op jit(solution)/shard_map/all_to_all | solution.py:46
  135.2 2.1 reduce.2
  138.2 2.2 convolution_bitcast_fusion.1
  142.8 11.6 %all-to-all-done = f32[128,1,1024]{2,1,0:T(1,128)} async-done(((f32[128,1,1024]{2,1,0:T(1,128)}), f32[128,1,1024]{2,1,0:T(1,128)}, u32[]{:S(2)}, u32[]{:S(2)}) %all-to-all-start) | async-done | bytes 524320 | tf_op jit(solution)/shard_map/all_to_all | solution.py:46
  154.4 4.3 all-to-all-start.3
  158.7 2.9 reduce
  165.5 3.1 all-to-all-done.3
  168.6 6.8 %all-to-all-start.1 = ((f32[128,1,1024]{2,1,0:T(1,128)}), f32[128,1,1024]{2,1,0:T(1,128)}, u32[]{:S(2)}, u32[]{:S(2)}) async-start(f32[128,1,1024]{2,1,0:T(1,128)} %reshape.79), calls=%async_computation.1 | async-start | bytes 1048576 | tf_op jit(solution)/shard_map/all_to_all | solution.py:49
  175.4 3.1 reduce.3
  180.2 15.5 %all-to-all-done.1 = f32[128,1,1024]{2,1,0:T(1,128)} async-done(((f32[128,1,1024]{2,1,0:T(1,128)}), f32[128,1,1024]{2,1,0:T(1,128)}, u32[]{:S(2)}, u32[]{:S(2)}) %all-to-all-start.1) | async-done | bytes 524320 | tf_op jit(solution)/shard_map/all_to_all | solution.py:49
  195.7 2.9 reduce.1
  201.2 93.5 %psum.36 = f32[1]{0:T(128)} all-reduce(f32[1]{0:T(128)} %bitcast.18), channel_id=1, replica_groups=mesh['ket'=128,'blk'=4] {'ket','blk'}, use_global_device_ids=true, to_apply=%region_3.0 | all-reduce | flops 1 | bytes 8 | tf_op jit(solution)/shard_map/psum | solution.py:35
  296.1 95.6 %psum.37 = f32[]{:T(128)} all-reduce(f32[]{:T(128)} %multiply_reduce_fusion.3), channel_id=1, replica_groups=mesh['ket'=128,'blk'=4] {'ket','blk'}, use_global_device_ids=true, to_apply=%region_5.0 | all-reduce | flops 1 | bytes 8 | tf_op jit(solution)/shard_map/psum | solution.py:39
  394.5 3.5 all-to-all-start.6
  399.8 7.1 %all-to-all-done.6 = f32[4,1,32768]{2,1,0:T(1,128)S(1)} async-done(((f32[4,1,32768]{2,1,0:T(1,128)}), f32[4,1,32768]{2,1,0:T(1,128)S(1)}, u32[]{:S(2)}, u32[]{:S(2)}) %all-to-all-start.6) | async-done | bytes 524320 | tf_op jit(solution)/shard_map/all_to_all | solution.py:28
  407.6 10.0 %all-to-all-start.4 = ((f32[128,1,1024]{2,1,0:T(1,128)}), f32[128,1,1024]{2,1,0:T(1,128)}, u32[]{:S(2)}, u32[]{:S(2)}) async-start(f32[128,1,1024]{2,1,0:T(1,128)} %reshape.85), calls=%async_computation.4 | async-start | bytes 1048576 | tf_op jit(solution)/shard_map/all_to_all | solution.py:46
  417.7 3.1 reduce.6
  421.6 2.2 convolution_bitcast_fusion
  425.6 2.7 reshape.91
  428.3 9.6 %all-to-all-done.4 = f32[128,1,1024]{2,1,0:T(1,128)} async-done(((f32[128,1,1024]{2,1,0:T(1,128)}), f32[128,1,1024]{2,1,0:T(1,128)}, u32[]{:S(2)}, u32[]{:S(2)}) %all-to-all-start.4) | async-done | bytes 524320 | tf_op jit(solution)/shard_map/all_to_all | solution.py:46
  437.9 4.3 all-to-all-start.7
  442.2 2.9 reduce.4
  452.0 6.8 all-to-all-start.5
  459.8 3.1 reduce.7
  466.1 13.1 %all-to-all-done.5 = f32[128,1,1024]{2,1,0:T(1,128)} async-done(((f32[128,1,1024]{2,1,0:T(1,128)}), f32[128,1,1024]{2,1,0:T(1,128)}, u32[]{:S(2)}, u32[]{:S(2)}) %all-to-all-start.5) | async-done | bytes 524320 | tf_op jit(solution)/shard_map/all_to_all | solution.py:49
  479.2 3.7 reduce.5
  485.4 2.3 multiply_reduce_fusion.2
  489.0 93.5 %psum.38 = f32[2]{0:T(128)S(1)} all-reduce(f32[2]{0:T(128)S(1)} %pad_maximum_fusion), channel_id=1, replica_groups=mesh['ket'=128,'blk'=4] {'ket','blk'}, use_global_device_ids=true, to_apply=%region_8.0 | all-reduce | flops 2 | bytes 16 | tf_op jit(solution)/shard_map/psum | solution.py:35
  585.2 95.4 %all-reduce.1 = (f32[]{:T(128)}, f32[8192]{0:T(1024)S(1)}) all-reduce(f32[]{:T(128)} %get-tuple-element.7, f32[8192]{0:T(1024)S(1)} %multiply_bitcast_fusion), channel_id=1, replica_groups=mesh['ket'=128,'blk'=4] {'ket','blk'}, use_global_device_ids=true, to_apply=%region_10.0 | all-reduce | flops 8193 | bytes 65544 | tf_op jit(solution)/shard_map/psum | solution.py:39
  (69 shorter events, 45.6 us)
Async XLA Ops:
  0.6 133.5 %copy-start = (f32[128,128]{1,0:T(8,128)S(1)}, f32[128,128]{1,0:T(8,128)}, u32[]{:S(2)}) copy-start(f32[128,128]{1,0:T(8,128)} %param.4) | copy-start | bytes 196612
  0.6 108.6 %copy-start.1 = (f32[64,16,128]{2,1,0:T(8,128)S(1)}, f32[64,16,128]{2,1,0:T(8,128)}, u32[]{:S(2)}) copy-start(f32[64,16,128]{2,1,0:T(8,128)} %param.3) | copy-start | bytes 1572868
  111.3 12.4 %all-to-all-start.2 = ((f32[4,1,32768]{2,1,0:T(1,128)}), f32[4,1,32768]{2,1,0:T(1,128)S(1)}, u32[]{:S(2)}, u32[]{:S(2)}) async-start(f32[4,1,32768]{2,1,0:T(1,128)} %reshape.81), calls=%async_computation.2 | async-start | bytes 1048576 | tf_op jit(solution)/shard_map/all_to_all | solution.py:28
  116.6 17.6 %copy-start.4 = (s32[128]{0:T(128)S(1)}, s32[128]{0:T(128)}, u32[]{:S(2)}) copy-start(s32[128]{0:T(128)} %param.5) | copy-start | bytes 1540
  123.7 30.7 %all-to-all-start = ((f32[128,1,1024]{2,1,0:T(1,128)}), f32[128,1,1024]{2,1,0:T(1,128)}, u32[]{:S(2)}, u32[]{:S(2)}) async-start(f32[128,1,1024]{2,1,0:T(1,128)} %reshape.77), calls=%async_computation | async-start | bytes 1048576 | tf_op jit(solution)/shard_map/all_to_all | solution.py:46
  154.4 14.2 %all-to-all-start.3 = ((f32[4,1,32768]{2,1,0:T(1,128)}), f32[4,1,32768]{2,1,0:T(1,128)}, u32[]{:S(2)}, u32[]{:S(2)}) async-start(f32[4,1,32768]{2,1,0:T(1,128)} %reshape.83), calls=%async_computation.3 | async-start | bytes 1048576 | tf_op jit(solution)/shard_map/all_to_all | solution.py:30
  168.6 27.2 %all-to-all-start.1 = ((f32[128,1,1024]{2,1,0:T(1,128)}), f32[128,1,1024]{2,1,0:T(1,128)}, u32[]{:S(2)}, u32[]{:S(2)}) async-start(f32[128,1,1024]{2,1,0:T(1,128)} %reshape.79), calls=%async_computation.1 | async-start | bytes 1048576 | tf_op jit(solution)/shard_map/all_to_all | solution.py:49
  198.9 1.0 copy-start.2
  394.5 12.4 %all-to-all-start.6 = ((f32[4,1,32768]{2,1,0:T(1,128)}), f32[4,1,32768]{2,1,0:T(1,128)S(1)}, u32[]{:S(2)}, u32[]{:S(2)}) async-start(f32[4,1,32768]{2,1,0:T(1,128)} %reshape.89), calls=%async_computation.6 | async-start | bytes 1048576 | tf_op jit(solution)/shard_map/all_to_all | solution.py:28
  406.8 0.8 copy-start.3
  407.6 30.2 %all-to-all-start.4 = ((f32[128,1,1024]{2,1,0:T(1,128)}), f32[128,1,1024]{2,1,0:T(1,128)}, u32[]{:S(2)}, u32[]{:S(2)}) async-start(f32[128,1,1024]{2,1,0:T(1,128)} %reshape.85), calls=%async_computation.4 | async-start | bytes 1048576 | tf_op jit(solution)/shard_map/all_to_all | solution.py:46
  437.9 14.2 %all-to-all-start.7 = ((f32[4,1,32768]{2,1,0:T(1,128)}), f32[4,1,32768]{2,1,0:T(1,128)}, u32[]{:S(2)}, u32[]{:S(2)}) async-start(f32[4,1,32768]{2,1,0:T(1,128)} %reshape.91), calls=%async_computation.7 | async-start | bytes 1048576 | tf_op jit(solution)/shard_map/all_to_all | solution.py:30
  452.0 27.2 %all-to-all-start.5 = ((f32[128,1,1024]{2,1,0:T(1,128)}), f32[128,1,1024]{2,1,0:T(1,128)}, u32[]{:S(2)}, u32[]{:S(2)}) async-start(f32[128,1,1024]{2,1,0:T(1,128)} %reshape.87), calls=%async_computation.5 | async-start | bytes 1048576 | tf_op jit(solution)/shard_map/all_to_all | solution.py:49
where the time goes:
time: 693 us; the launch traced here: 683 us
  blocking collectives  484 us (70%)
  waiting for transfers between devices  68.2 us (10%)
  starting transfers between devices  49.7 us (7%)
  local copies, waits for them, and re-layouts  33.8 us (5%)
  other arithmetic  31.4 us (5%)
  matrix products  12.3 us (2%)
    psum x2, blocking collectives, krylov_step(): lax.psum(jnp.sum(residual * residual), ('ket', 'blk')) / entries  191 us
    psum x2, blocking collectives, krylov_step(): correlation = lax.psum(local_dots, ('ket', 'blk')) / entries  187 us
    psum x1, blocking collectives, shards(): norm_start = lax.psum(jnp.sum(density * density), ('ket', 'blk'))  106 us
    all_to_all x2, waiting for transfers between devices, liouvillian(): lax.all_to_all(ket_part(turned), 'ket', split_axis=0, concat_axis=1, tile...  28.6 us
    all_to_all x2, waiting for transfers between devices, liouvillian(): lax.all_to_all(tensor.reshape(pair_rows, -1), 'ket', split_axis=1, concat...  21.2 us
    all_to_all x2, starting transfers between devices, liouvillian(): lax.all_to_all(tensor.reshape(pair_rows, -1), 'ket', split_axis=1, concat...  20.5 us
    unnamed x27, local copies, waits for them, and re-layouts  19.1 us
    all_to_all x2, waiting for transfers between devices, bra_part(): lax.all_to_all(tensor, 'blk', split_axis=2, concat_axis=1, tiled=True)  14.1 us
  transfers between devices with their start and end apart: 8, of which 8 were waited for; matrix products, arithmetic and copies ran while one was open for 7% of the time, Pallas kernels for 0%

commit v1 on v0

v1 whole, which is shorter than its diff:
```python
import jax
import jax.numpy as jnp
from jax import lax
from jax.experimental import pallas as pl
from jax.experimental.pallas import tpu as pltpu
from jax.sharding import PartitionSpec as P


AXES = ("ket", "blk")
LANES = 128
HIGHEST = lax.Precision.HIGHEST
F32 = jnp.float32


def dot(a, b):
    return jnp.dot(a, b, precision=HIGHEST, preferred_element_type=F32)


def iota(shape, axis):
    return lax.broadcasted_iota(jnp.int32, shape, axis)


def vmem_call(body, shapes, name, n_vmem, n_smem=0, scratch=()):
    in_specs = [pl.BlockSpec(memory_space=pltpu.SMEM)] * n_smem
    in_specs += [pl.BlockSpec(memory_space=pltpu.VMEM)] * n_vmem
    return pl.pallas_call(
        body,
        out_shape=[jax.ShapeDtypeStruct(shape, F32) for shape in shapes],
        in_specs=in_specs,
        out_specs=[pl.BlockSpec(memory_space=pltpu.VMEM)] * len(shapes),
        scratch_shapes=list(scratch),
        name=name,
    )


def send_body(x_ref, out_ref):
    for c in range(8):
        out_ref[pl.ds(c, 128, stride=8), :] = x_ref[c * 128:(c + 1) * 128, :].T


def apply_d(x_ref, shifted, window, wide_ref, out_ref):
    for k in range(16):
        wide_ref[:, k * 128:(k + 1) * 128] = x_ref[pl.ds(k, 64, stride=16), :]
    wide_ref[...] = dot(window, wide_ref[...])
    for k in range(16):
        out_ref[pl.ds(k, 64, stride=16), :] = wide_ref[:, k * 128:(k + 1) * 128]
    out_ref[...] += dot(x_ref[...], shifted)


def prep_body(x_ref, decay_ref, order_ref, dx_ref, g_ref, shifted_ref, kron_ref, tau_ref, wide_ref):
    onehot = (order_ref[...] == iota((128, 128), 1)).astype(F32)
    g = dot(dot(onehot, decay_ref[...]), onehot.T)
    g_ref[...] = g
    rows, cols = iota((128, 128), 0), iota((128, 128), 1)
    weight = jnp.where(rows < 64, 2.0 / 128 + 2.0 / 64, 2.0 / 128)
    tau = jnp.sum(jnp.where(rows == cols, g * weight, 0.0), keepdims=True)
    tau_ref[...] = jnp.broadcast_to(tau, (8, 128))
    shifted = jnp.where(rows == cols, g - tau, g)
    shifted_ref[...] = shifted
    window = g[:64, :64]
    r512, c64 = iota((512, 64), 0), iota((512, 64), 1)
    spread = (c64 == (r512 // 128) * 16 + r512 % 16).astype(F32)
    full = dot(dot(spread, window), spread.T)
    r, c = iota((512, 512), 0), iota((512, 512), 1)
    kron_ref[...] = jnp.where((r // 16) % 8 == (c // 16) % 8, full, 0.0)
    apply_d(x_ref, shifted, window, wide_ref, dx_ref)


def turned_body(y_ref, g_ref, kron_ref, out_ref, jump_ref, cat_ref):
    g = g_ref[...]
    lane, col = iota((64, 128), 1), iota((64, 128), 0)
    jump = [jnp.zeros((1, 128), F32) for _ in range(2)]
    for kb in range(4):
        spread = (col == kb * 16 + lane % 16).astype(F32)
        weights = dot(g[:, :64], spread)
        for h in range(2):
            piece = y_ref[pl.ds(kb * 2 + h, 128, stride=8), :]
            cat_ref[h * 128:(h + 1) * 128, kb * 128:(kb + 1) * 128] = piece
            jump[h] += jnp.sum(weights * piece, axis=0, keepdims=True)
    jump_ref[...] = jnp.concatenate(jump + [jnp.zeros((6, 128), F32)], axis=0)

    def apply_c(cat):
        both = jnp.concatenate([dot(g, cat[:128]), dot(g, cat[128:])], axis=0)
        return both + dot(cat, kron_ref[...])

    for v in range(2):
        cat_ref[...] = apply_c(cat_ref[...])
        for kb in range(4):
            for h in range(2):
                out_ref[pl.ds(kb * 4 + v * 2 + h, 128, stride=16), :] = (
                    cat_ref[h * 128:(h + 1) * 128, kb * 128:(kb + 1) * 128]
                )


def moments_body(r_ref, x_ref, dx_ref, shifted_ref, g_ref, jump_ref, w_ref, z_ref, msg_ref, wide_ref, t_ref):
    for c in range(8):
        part = slice(c * 128, (c + 1) * 128)
        cx = r_ref[pl.ds((c // 2) * 4 + c % 2, 128, stride=16), :].T
        w_ref[part, :] = dx_ref[part, :] + cx
        t_ref[part, :] = dx_ref[part, :] + 2.0 * cx
    apply_d(t_ref, shifted_ref[...], g_ref[:64, :64], wide_ref, z_ref)
    for c in range(8):
        part = slice(c * 128, (c + 1) * 128)
        z_ref[part, :] += r_ref[pl.ds((c // 2) * 4 + 2 + c % 2, 128, stride=16), :].T
    x, w, z = x_ref[...], w_ref[...], z_ref[...]
    lane = iota((1, 128), 1)
    row = jnp.zeros((1, 128), F32)
    for slot, product in enumerate((x * x, x * w, w * w, w * z, z * z)):
        row = jnp.where(lane == slot, jnp.sum(product, keepdims=True), row)
    n, at = iota((512, 128), 0), iota((512, 128), 1)
    jump = jnp.where((n // 64) % 2 == 0, jump_ref[0:1, :], jump_ref[1:2, :])
    picked = jnp.sum(jnp.where(at // 16 == (n // 8) % 8, jump, 0.0), axis=1, keepdims=True)
    msg_ref[...] = jnp.where(at == 5, picked * (1.0 / 128), jnp.broadcast_to(row, (512, 128)))


def finish_body(me_ref, msg_ref, x_ref, w_ref, z_ref, tau_ref, out_ref, coeff_ref, jump_ref):
    msg = msg_ref[...]
    total = jnp.sum(msg, axis=0, keepdims=True)
    lane = iota((1, 128), 1)

    def pick(slot):
        return jnp.sum(jnp.where(lane == slot, total, 0.0), keepdims=True)

    m0, m1, m2, m3, m4 = (pick(slot) for slot in range(5))
    m1, m2, m3, m4 = m1 / m0, m2 / m0, m3 / m0, m4 / m0
    tau = tau_ref[0:1, 0:1]
    beta1_sq = m2 - m1 * m1
    beta1 = jnp.sqrt(beta1_sq)
    alpha1 = (m3 - 2.0 * m1 * m2 + m1 * m1 * m1) / beta1_sq
    norm_sq = (m4 - 2.0 * m1 * m3 + m1 * m1 * m2) / beta1_sq
    beta2 = jnp.sqrt(norm_sq - beta1_sq - alpha1 * alpha1)
    scale = lax.rsqrt(m0 * (1.0 / 67108864.0)) / (beta1 * beta2)
    on_x = (alpha1 * m1 - beta1_sq) * scale
    on_w = (m1 + alpha1) * scale
    out_ref[...] = z_ref[...] * scale - w_ref[...] * on_w + x_ref[...] * on_x
    values = (-0.5 * (m1 + tau), 0.5 * beta1, 0.5 * beta1, -0.5 * (alpha1 + tau), 0.5 * beta2)
    row = jnp.zeros((1, 128), F32)
    for slot, value in enumerate(values):
        row = jnp.where(lane == slot, value, row)
    coeff_ref[...] = jnp.broadcast_to(row, (8, 128))
    me = me_ref[0]
    s, t = iota((512, 128), 0), iota((512, 128), 1)
    source = ((me % 8) * 16 + t) * 4 + me // 128
    mine = jnp.sum(jnp.where(t == 5, msg, 0.0), axis=1, keepdims=True)
    found = jnp.sum(jnp.where(s == source, mine, 0.0), axis=0, keepdims=True)
    jump_ref[...] = jnp.broadcast_to(found, (8, 128))


def shards(density, decay_matrix, atom_order):
    x = density.reshape(1024, 128)
    wide = pltpu.VMEM((64, 2048), F32)

    def exchange(rows):
        return lax.all_to_all(rows, AXES, split_axis=0, concat_axis=0, tiled=True)

    (sent,) = vmem_call(send_body, [(1024, 128)], "send", 1)(x)
    turned = exchange(sent)
    dx, g, shifted, kron, tau = vmem_call(
        prep_body,
        [(1024, 128), (128, 128), (128, 128), (512, 512), (8, 128)],
        "prep", 3, scratch=[wide],
    )(x, decay_matrix, atom_order.reshape(128, 1))
    images, jump_row = vmem_call(
        turned_body, [(2048, 128), (8, 128)], "turned", 3,
        scratch=[pltpu.VMEM((256, 512), F32)],
    )(turned, g, kron)
    returned = exchange(images)
    w, z, message = vmem_call(
        moments_body, [(1024, 128), (1024, 128), (512, 128)], "moments", 6,
        scratch=[wide, pltpu.VMEM((1024, 128), F32)],
    )(returned, x, dx, shifted, g, jump_row)
    received = exchange(message)
    me = lax.axis_index("ket") * 4 + lax.axis_index("blk")
    out, coeffs, jump = vmem_call(
        finish_body, [(1024, 128), (8, 128), (8, 128)], "finish", 5, n_smem=1
    )(me.astype(jnp.int32).reshape(1), received, x, w, z, tau)
    return out.reshape(density.shape), coeffs[0, :5], jump[0, :16]


def solution(mesh):
    return jax.shard_map(
        shards,
        mesh=mesh,
        in_specs=(P("ket", "blk", None), P(), P()),
        out_specs=(P("ket", "blk", None), P(), P(("ket", "blk"))),
        check_vma=False,
    )
```

time: 693 us -> 133 us (0.19); the launches traced: 683 us -> 132 us
  blocking collectives: 484 us -> 44.2 us
  waiting for transfers between devices: 68.2 us -> 31.3 us
  other arithmetic: 31.4 us -> 0 us
  local copies, waits for them, and re-layouts: 33.8 us -> 5.27 us
  Pallas kernels: 0 us -> 19.2 us
  starting transfers between devices: 49.7 us -> 31.5 us
  matrix products: 12.3 us -> 0 us
    psum x5 -> x0, blocking collectives: 484 us -> none  [the longest x2 191 us: krylov_step(): lax.psum(jnp.sum(residual * residual), ('ket', 'blk')) / entries]
    all_to_all x0 -> x1, blocking collectives: none -> 44.2 us  [exchange(): return lax.all_to_all(rows, AXES, split_axis=0, concat_axis=0, tiled=True)]
    all_to_all x8 -> x2, waiting for transfers between devices: 68.2 us -> 31.3 us  [exchange(): return lax.all_to_all(rows, AXES, split_axis=0, concat_axis=0, tiled=True)]
    all_to_all x8 -> x0, other arithmetic: 23.8 us -> none  [the longest x2 6.65 us: liouvillian(): lax.all_to_all(ket_part(turned), 'ket', split_axis=0, concat_axis=1, tile...]
    pallas_call x0 -> x5, Pallas kernels: none -> 19.2 us  [the longest x1 5.73 us: shards(): vmem_call(turned_body, [(2048, 128), (8, 128)], 'turned', 3, scratch=[plt...]
    all_to_all x8 -> x2, starting transfers between devices: 49.7 us -> 31.5 us  [exchange(): return lax.all_to_all(rows, AXES, split_axis=0, concat_axis=0, tiled=True)]
    unnamed x27 -> x6, local copies, waits for them, and re-layouts: 19.1 us -> 2.15 us
    dot_general x12 -> x0, matrix products: 12.3 us -> none  [the longest x2 4.4 us: bra_part(): mixed_rows = jnp.einsum('kb,pbc->pkc', window, turned, precision=highest)]
  transfers between devices with their start and end apart: 8 -> 2, of which waited for: 8 -> 2; matrix products, arithmetic and copies ran while one was open for 7% -> 1% of each run, Pallas kernels for 0% -> 4%
where the time goes in v1:
time: 133 us; the launch traced here: 132 us
  blocking collectives  44.2 us (33%)
  starting transfers between devices  31.5 us (24%)
  waiting for transfers between devices  31.3 us (24%)
  Pallas kernels  19.2 us (14%)
  local copies, waits for them, and re-layouts  5.27 us (4%)
    all_to_all x1, blocking collectives, exchange(): return lax.all_to_all(rows, AXES, split_axis=0, concat_axis=0, tiled=True)  44.2 us
    all_to_all x2, starting transfers between devices, exchange(): return lax.all_to_all(rows, AXES, split_axis=0, concat_axis=0, tiled=True)  31.5 us
    all_to_all x2, waiting for transfers between devices, exchange(): return lax.all_to_all(rows, AXES, split_axis=0, concat_axis=0, tiled=True)  31.3 us
    pallas_call x1, Pallas kernels, shards(): vmem_call(turned_body, [(2048, 128), (8, 128)], 'turned', 3, scratch=[plt...  5.73 us
    pallas_call x1, Pallas kernels, shards(): vmem_call(prep_body, [(1024, 128), (128, 128), (128, 128), (512, 512), (8...  4.92 us
    pallas_call x1, Pallas kernels, shards(): vmem_call(moments_body, [(1024, 128), (1024, 128), (512, 128)], 'moments'...  3.87 us
  transfers between devices with their start and end apart: 2, of which 2 were waited for; matrix products, arithmetic and copies ran while one was open for 1% of the time, Pallas kernels for 4%

profile of v1, /device:TPU:1, one launch (start us, length us, event | category | flops | bytes accessed | tf_op | source)
XLA Modules:
  0.0 132.2 jit_solution(11249532327763256725)
XLA Ops:
  0.6 2.0 %send.1 = f32[1024,128]{1,0:T(8,128)} custom-call(f32[1024,128]{1,0:T(8,128)} %bitcast.16), custom_call_target="tpu_custom_call" | custom-call | tf_op jit(solution)/shard_map/send/pallas_call | solution.py:156
  2.7 22.1 %all-to-all-start = ((f32[512,2,128]{2,1,0:T(2,128)}), f32[512,2,128]{2,1,0:T(2,128)S(1)}, u32[]{:S(2)}, u32[]{:S(2)}) async-start(f32[512,2,128]{2,1,0:T(2,128)} %bitcast.22), calls=%async_computation | async-start | bytes 1048576 | tf_op jit(solution)/shard_map/all_to_all | solution.py:154
  24.8 0.0 copy-start.2
  24.8 0.6 copy-done.2
  25.5 0.7 copy.7.order_ref
  26.2 4.9 %prep.1 = (f32[1024,128]{1,0:T(8,128)}, f32[128,128]{1,0:T(8,128)}, f32[128,128]{1,0:T(8,128)}, f32[512,512]{1,0:T(8,128)}, f32[8,128]{1,0:T(8,128)}) custom-call(f32[1024,128]{1,0:T(8,128)} %bitcast.17, f32[128,128]{1,0:T(8,128)} %decay_ref.1, s32[128,1]{1,0:T(8,128)} %copy.7.order_ref), custom_call_target="tpu_custom_call" | custom-call | tf_op jit(solution)/shard_map/prep/pallas_call | solution.py:158
  31.2 14.9 %all-to-all-done = f32[512,2,128]{2,1,0:T(2,128)S(1)} async-done(((f32[512,2,128]{2,1,0:T(2,128)}), f32[512,2,128]{2,1,0:T(2,128)S(1)}, u32[]{:S(2)}, u32[]{:S(2)}) %all-to-all-start) | async-done | bytes 524320 | tf_op jit(solution)/shard_map/all_to_all | solution.py:154
  46.1 0.0 copy-start
  46.1 0.8 copy-done
  46.9 5.7 %turned.1 = (f32[2048,128]{1,0:T(8,128)}, f32[8,128]{1,0:T(8,128)}) custom-call(f32[1024,128]{1,0:T(8,128)} %bitcast.21, f32[128,128]{1,0:T(8,128)} %get-tuple-element.16.g_ref, f32[512,512]{1,0:T(8,128)} %get-tuple-element.17.kron_ref), custom_call_target="tpu_custom_call" | custom-call | tf_op jit(solution)/shard_map/turned/pallas_call | solution.py:163
  52.6 44.2 %all_to_all.33 = f32[512,4,128]{2,1,0:T(4,128)} all-to-all(f32[512,4,128]{2,1,0:T(4,128)} %bitcast.23), channel_id=1, replica_groups=mesh['ket'=128,'blk'=4] {'ket','blk'}, dimensions={0} | all-to-all | bytes 2097152 | tf_op jit(solution)/shard_map/all_to_all | solution.py:154
  96.8 3.9 %moments.1 = (f32[1024,128]{1,0:T(8,128)}, f32[1024,128]{1,0:T(8,128)}, f32[512,128]{1,0:T(8,128)}) custom-call(f32[2048,128]{1,0:T(8,128)} %bitcast.20, f32[1024,128]{1,0:T(8,128)} %bitcast.18, f32[1024,128]{1,0:T(8,128)} %get-tuple-element.19.dx_ref, f32[128,128]{1,0:T(8,128)} %get-tuple-element.20.shifted_ref, f32[128,128]{1,0:T(8,128)} %get-tuple-element.16.g_ref, ...), custom_call_target="tpu_custom_call" | custom-call | tf_op jit(solution)/shard_map/moments/pallas_call | solution.py:168
  100.7 9.3 %all-to-all-start.2 = ((f32[512,1,128]{2,1,0:T(1,128)}), f32[512,1,128]{2,1,0:T(1,128)S(1)}, u32[]{:S(2)}, u32[]{:S(2)}) async-start(f32[512,1,128]{2,1,0:T(1,128)} %bitcast.25), calls=%async_computation.2 | async-start | bytes 524288 | tf_op jit(solution)/shard_map/all_to_all | solution.py:154
  110.1 16.4 %all-to-all-done.2 = f32[512,1,128]{2,1,0:T(1,128)S(1)} async-done(((f32[512,1,128]{2,1,0:T(1,128)}), f32[512,1,128]{2,1,0:T(1,128)S(1)}, u32[]{:S(2)}, u32[]{:S(2)}) %all-to-all-start.2) | async-done | bytes 262176 | tf_op jit(solution)/shard_map/all_to_all | solution.py:154
  126.5 0.0 copy-start.1
  126.5 0.7 copy-done.1
  127.2 2.7 %finish.1 = (f32[1024,128]{1,0:T(8,128)}, f32[8,128]{1,0:T(8,128)}, f32[8,128]{1,0:T(8,128)}) custom-call(s32[1]{0:T(128)} %bitcast.me_ref, f32[512,128]{1,0:T(8,128)} %bitcast.24, f32[1024,128]{1,0:T(8,128)} %bitcast.19, f32[1024,128]{1,0:T(8,128)} %get-tuple-element.23.w_ref, f32[1024,128]{1,0:T(8,128)} %get-tuple-element.24.z_ref, ...), custom_call_target="tpu_custom_call" | custom-call | tf_op jit(solution)/shard_map/finish/pallas_call | solution.py:174
  129.8 1.2 slice_bitcast_fusion
  131.0 1.2 slice_bitcast_fusion.1
Async XLA Ops:
  2.7 43.4 %all-to-all-start = ((f32[512,2,128]{2,1,0:T(2,128)}), f32[512,2,128]{2,1,0:T(2,128)S(1)}, u32[]{:S(2)}, u32[]{:S(2)}) async-start(f32[512,2,128]{2,1,0:T(2,128)} %bitcast.22), calls=%async_computation | async-start | bytes 1048576 | tf_op jit(solution)/shard_map/all_to_all | solution.py:154
  24.8 0.7 copy-start.2
  46.1 0.8 copy-start
  100.7 25.8 %all-to-all-start.2 = ((f32[512,1,128]{2,1,0:T(1,128)}), f32[512,1,128]{2,1,0:T(1,128)S(1)}, u32[]{:S(2)}, u32[]{:S(2)}) async-start(f32[512,1,128]{2,1,0:T(1,128)} %bitcast.25), calls=%async_computation.2 | async-start | bytes 524288 | tf_op jit(solution)/shard_map/all_to_all | solution.py:154
  126.5 0.7 copy-start.1
